TPU v7x, 32 devices: a whole 2x2x4 slice. The times are simulated.
32 devices in a mesh: dp: 16 (over z, y, core), mp: 2 (over x).
Axes of the slice: x: 2, y: 2, z: 4, core: 2. Of those that a mesh axis runs over, the one named last changes fastest.
Arguments:
- tokens_in: bfloat16 [4096, 2048], P(('dp', 'mp')), may hold values from -6 to 6
- teacher: bfloat16 [4096, 2048], P(('dp', 'mp')), may hold values from -6 to 6
- valid_mask: int32 [16, 256], P('dp', 'mp'), may hold values from 0 to 1, as said below
- group_of: int32 [16], replicated, may hold values from 0 to 1, as said below
- prompt_len: int32 [2], replicated, may hold values from 128 to 256
- ln1_gain: bfloat16 [2048], P('dp'), may hold values from 0.5 to 1.5
- ln1_bias: bfloat16 [2048], P('dp'), may hold values from -2 to 2
- w_query: bfloat16 [2048, 2048], P('dp', 'mp'), may hold values from -0.125 to 0.125
- w_key: bfloat16 [2048, 2048], P('dp', 'mp'), may hold values from -0.125 to 0.125
- w_value: bfloat16 [2048, 4096], P('dp', 'mp'), may hold values from -0.125 to 0.125
- w_gate: bfloat16 [2048, 4096], P('dp', 'mp'), may hold values from -0.125 to 0.125
- w_out: bfloat16 [2048, 4096], P('dp', 'mp'), may hold values from -0.1875 to 0.1875
- ln2_gain: bfloat16 [2048], P('dp'), may hold values from 0.5 to 1.5
- ln2_bias: bfloat16 [2048], P('dp'), may hold values from -2 to 2
- w_up: bfloat16 [2048, 4096], P('dp', 'mp'), may hold values from -0.125 to 0.125
- w_down: bfloat16 [2048, 4096], P('dp', 'mp'), may hold values from -0.125 to 0.125
Outputs:
- block_out: float32 [4096, 2048], P(('dp', 'mp'))
- grad_tokens: float32 [4096, 2048], P(('dp', 'mp'))
- loss: float32 [], replicated
- grad_ln1_gain: float32 [2048], P('dp')
- grad_ln1_bias: float32 [2048], P('dp')
- grad_w_query: float32 [2048, 2048], P('dp', 'mp')
- grad_w_key: float32 [2048, 2048], P('dp', 'mp')
- grad_w_value: float32 [2048, 4096], P('dp', 'mp')
- grad_w_gate: float32 [2048, 4096], P('dp', 'mp')
- grad_w_out: float32 [2048, 4096], P('dp', 'mp')
- grad_ln2_gain: float32 [2048], P('dp')
- grad_ln2_bias: float32 [2048], P('dp')
- grad_w_up: float32 [2048, 4096], P('dp', 'mp')
- grad_w_down: float32 [2048, 4096], P('dp', 'mp')
Inputs may be any that keep to these rules, and one draw needn't show every extreme that they name: `valid_mask`: in each row the ones form a leading run of one or more positions, zeros follow. `group_of`: each group number is held by exactly 8 segments; a group's prompt is its lowest-numbered segment, the others are its continuations.
All inputs are finite; a program needn't handle non-finite values.
Results may differ from a plain program's by a relative error of at most 0.013.
Values may be sent and summed in bfloat16 or wider, within the bound.
A program may use at most 192 MiB of HBM per device.

v0:
```python
import math
import jax
import jax.numpy as jnp
from jax import lax
from jax.sharding import PartitionSpec as P

DK = 256
DV = 512
EPSILON = 1e-05
GROUP_EPSILON = 0.05


def norm_stats(values, floor_eps):
    center = jnp.mean(values, axis=-1, keepdims=True)
    shifted = values - center
    inv_std = lax.rsqrt(jnp.mean(shifted * shifted, axis=-1, keepdims=True) + floor_eps)
    return (shifted * inv_std, inv_std)


def norm_back(grad_in, normed, inv_std):
    mean_grad = jnp.mean(grad_in, axis=-1, keepdims=True)
    mean_proj = jnp.mean(grad_in * normed, axis=-1, keepdims=True)
    return (grad_in - mean_grad - normed * mean_proj) * inv_std


def xpos_tables(positions, direction):
    half_dim = DK // 2
    pair_index = jnp.arange(half_dim, dtype=jnp.float32)
    frequency = jnp.exp(-(2.0 * pair_index / DK) * math.log(10000.0))
    base_ratio = (2.0 * pair_index / DK + 0.4) / 1.4
    angles = positions[:, None] * frequency[None, :]
    factor = jnp.exp(direction * (positions[:, None] / 512.0) * jnp.log(base_ratio)[None, :])
    return (jnp.cos(angles), jnp.sin(angles), factor)


def rotate_pairs(values, cosine, sine_tab, factor):
    half_dim = values.shape[-1] // 2
    first_half = values[..., :half_dim]
    second = values[..., half_dim:]
    cosine = cosine[:, None, :]
    sine_tab = sine_tab[:, None, :]
    factor = factor[:, None, :]
    return jnp.concatenate(
        [
            (first_half * cosine - second * sine_tab) * factor,
            (second * cosine + first_half * sine_tab) * factor,
        ],
        axis=-1,
    )


def rotate_back(grad_rot, cosine, sine_tab, factor):
    half_dim = grad_rot.shape[-1] // 2
    first_half = grad_rot[..., :half_dim]
    second = grad_rot[..., half_dim:]
    cosine = cosine[:, None, :]
    sine_tab = sine_tab[:, None, :]
    factor = factor[:, None, :]
    return jnp.concatenate(
        [
            (first_half * cosine + second * sine_tab) * factor,
            (second * cosine - first_half * sine_tab) * factor,
        ],
        axis=-1,
    )


def plain_dot(first_op, second_op):
    return jnp.dot(first_op, second_op, preferred_element_type=jnp.float32)


def contract_last(first_op, second_op):
    return lax.dot_general(
        first_op, second_op, (((1,), (1,)), ((), ())), preferred_element_type=jnp.float32
    )


def contract_first(first_op, second_op):
    return lax.dot_general(
        first_op, second_op, (((0,), (0,)), ((), ())), preferred_element_type=jnp.float32
    )


def gather_rows(rows_low):
    return lax.all_gather(rows_low, "mp", axis=0, tiled=True)


def scatter_rows(terms):
    return lax.psum_scatter(terms, "mp", scatter_dimension=0, tiled=True)


def on_device(
    tokens_in,
    teacher,
    valid_mask,
    group_of,
    prompt_len,
    ln1_gain,
    ln1_bias,
    w_query,
    w_key,
    w_value,
    w_gate,
    w_out,
    ln2_gain,
    ln2_bias,
    w_up,
    w_down,
):
    half_rows = tokens_in.shape[0]
    model_dim = tokens_in.shape[1]
    seg_len = half_rows * lax.axis_size("mp")
    seg_count = group_of.shape[0]
    group_count = prompt_len.shape[0]
    heads_local = w_query.shape[1] // DK
    token_total = seg_len * seg_count
    dp_index = lax.axis_index("dp")
    mp_index = lax.axis_index("mp")
    attn_full = (
        lax.all_gather(ln1_gain, "dp", axis=0, tiled=True),
        lax.all_gather(ln1_bias, "dp", axis=0, tiled=True),
        lax.all_gather(w_query, "dp", axis=0, tiled=True),
        lax.all_gather(w_key, "dp", axis=0, tiled=True),
        lax.all_gather(w_value, "dp", axis=0, tiled=True),
        lax.all_gather(w_gate, "dp", axis=0, tiled=True),
        lax.all_gather(w_out, "dp", axis=0, tiled=True),
    )
    ffn_full = (
        lax.all_gather(ln2_gain, "dp", axis=0, tiled=True),
        lax.all_gather(ln2_bias, "dp", axis=0, tiled=True),
        lax.all_gather(w_up, "dp", axis=0, tiled=True),
        lax.all_gather(w_down, "dp", axis=0, tiled=True),
    )
    gain_one = attn_full[0].astype(jnp.float32)
    bias_one = attn_full[1].astype(jnp.float32)
    wq_full, wk_full, wv_full, wg_full, wo_full = (
        attn_full[2],
        attn_full[3],
        attn_full[4],
        attn_full[5],
        attn_full[6],
    )
    gain_two = ffn_full[0].astype(jnp.float32)
    bias_two = ffn_full[1].astype(jnp.float32)
    wu_full, wd_full = (ffn_full[2], ffn_full[3])
    segment_ids = jnp.arange(seg_count, dtype=jnp.int32)
    my_group = jnp.sum(jnp.where(segment_ids == dp_index, group_of, 0))
    first_member = jnp.min(jnp.where(group_of == my_group, segment_ids, seg_count))
    prompt_flag = (first_member == dp_index).astype(jnp.float32)
    group_match = jnp.arange(group_count, dtype=jnp.int32) == my_group
    group_onehot = group_match.astype(jnp.float32)
    prompt_size = jnp.sum(jnp.where(group_match, prompt_len, 0))
    token_ids = jnp.arange(seg_len, dtype=jnp.int32)
    offset = jnp.where(prompt_flag > 0, 0, prompt_size)
    positions = (token_ids + offset).astype(jnp.float32)
    head_ids = (mp_index * heads_local + jnp.arange(heads_local, dtype=jnp.int32)).astype(
        jnp.float32
    )
    log_decay = jnp.log(1.0 - 2.0 ** (-5.0 - head_ids))
    before_end = token_ids < prompt_size
    state_age = (prompt_size - 1 - token_ids).astype(jnp.float32)
    state_weighting = jnp.where(
        (before_end & (prompt_flag > 0))[:, None],
        jnp.exp(log_decay[None, :] * jnp.maximum(state_age, 0.0)[:, None]),
        0.0,
    )
    continuation_factor = (1.0 - prompt_flag) * jnp.exp(
        log_decay[None, :] * (token_ids.astype(jnp.float32) + 1.0)[:, None]
    )
    float_ids = token_ids.astype(jnp.float32)
    distance = float_ids[:, None] - float_ids[None, :]
    decay_mat = jnp.where(
        distance[None] >= 0.0,
        jnp.exp(log_decay[:, None, None] * jnp.maximum(distance, 0.0)[None]),
        0.0,
    )
    own_ids = mp_index * half_rows + jnp.arange(half_rows, dtype=jnp.int32)
    loss_mask = valid_mask[0].astype(jnp.float32) * jnp.where(
        prompt_flag > 0, own_ids < prompt_size, True
    ).astype(jnp.float32)
    token_rows = tokens_in.astype(jnp.float32)
    normed_one, inv_one = norm_stats(token_rows, EPSILON)
    a_all = gather_rows((normed_one * gain_one + bias_one).astype(jnp.bfloat16))
    queries = plain_dot(a_all, wq_full).reshape(seg_len, heads_local, DK)
    keys_raw = plain_dot(a_all, wk_full).reshape(seg_len, heads_local, DK)
    reduced_values = (
        plain_dot(a_all, wv_full).astype(jnp.bfloat16).reshape(seg_len, heads_local, DV)
    )
    gate_pre = plain_dot(a_all, wg_full)
    cosine, sine_tab, grow_fac = xpos_tables(positions, 1.0)
    _, _, shrink = xpos_tables(positions, -1.0)
    q_scale = DK ** (-0.5)
    rotated_queries = (rotate_pairs(queries, cosine, sine_tab, grow_fac) * q_scale).astype(
        jnp.bfloat16
    )
    rotated_keys = rotate_pairs(keys_raw, cosine, sine_tab, shrink).astype(jnp.bfloat16)
    local_state = jnp.einsum(
        "jld,jla->lda",
        rotated_keys.astype(jnp.float32) * state_weighting[:, :, None],
        reduced_values.astype(jnp.float32),
        precision=lax.Precision.HIGHEST,
    )
    slots = group_onehot[:, None, None, None] * (prompt_flag * local_state)[None]
    summed = lax.psum(slots, "dp")
    state_lookup = jnp.sum(summed * group_onehot[:, None, None, None], axis=0).astype(jnp.bfloat16)
    scores = jnp.einsum(
        "thk,nhk->htn", rotated_queries, rotated_keys, preferred_element_type=jnp.float32
    )
    weights_low = (scores * decay_mat).astype(jnp.bfloat16)
    retained_output = jnp.einsum(
        "htn,nhv->thv", weights_low, reduced_values, preferred_element_type=jnp.float32
    )
    carried_forward = jnp.einsum(
        "ozi,ziw->ozw", rotated_queries, state_lookup, preferred_element_type=jnp.float32
    )
    retained_output = retained_output + continuation_factor[:, :, None] * carried_forward
    grouped, inv_group = norm_stats(retained_output, GROUP_EPSILON)
    gate_act = jax.nn.silu(gate_pre).reshape(seg_len, heads_local, DV)
    gated_out = (gate_act * grouped).reshape(seg_len, heads_local * DV).astype(jnp.bfloat16)
    attn_own = scatter_rows(contract_last(gated_out, wo_full))
    hidden_res = token_rows + attn_own
    normed_two, inv_two = norm_stats(hidden_res, EPSILON)
    c_all = gather_rows((normed_two * gain_two + bias_two).astype(jnp.bfloat16))
    up_pre = plain_dot(c_all, wu_full)
    up_act = jax.nn.gelu(up_pre, approximate=False).astype(jnp.bfloat16)
    ffn_own = scatter_rows(contract_last(up_act, wd_full))
    block_out = hidden_res + ffn_own
    error_rows = block_out - teacher.astype(jnp.float32)
    weighted = loss_mask[:, None] * error_rows
    valid_count, squared = lax.psum(
        (jnp.sum(loss_mask), jnp.sum(weighted * error_rows)), ("dp", "mp")
    )
    grad_out = token_total / valid_count * weighted
    loss_value = squared / (valid_count * model_dim)
    grad_ffn_all = gather_rows(grad_out.astype(jnp.bfloat16))
    grad_up_act = plain_dot(grad_ffn_all, wd_full)
    _, gelu_pull = jax.vjp(lambda inner: jax.nn.gelu(inner, approximate=False), up_pre)
    grad_up = gelu_pull(grad_up_act)[0].astype(jnp.bfloat16)
    grad_wd = contract_first(grad_ffn_all, up_act)
    grad_wu = contract_first(c_all, grad_up)
    grad_c = scatter_rows(contract_last(grad_up, wu_full))
    grad_gain2_part = jnp.sum(grad_c * normed_two, axis=0)
    grad_bias2_part = jnp.sum(grad_c, axis=0)
    grad_hidden = grad_out + norm_back(grad_c * gain_two, normed_two, inv_two)
    ffn_reduced = (
        lax.psum_scatter(grad_gain2_part, "dp", scatter_dimension=0, tiled=True),
        lax.psum_scatter(grad_bias2_part, "dp", scatter_dimension=0, tiled=True),
        lax.psum_scatter(grad_wu, "dp", scatter_dimension=0, tiled=True),
        lax.psum_scatter(grad_wd, "dp", scatter_dimension=0, tiled=True),
    )
    grad_attn_all = gather_rows(grad_hidden.astype(jnp.bfloat16))
    grad_gated = plain_dot(grad_attn_all, wo_full).reshape(seg_len, heads_local, DV)
    grad_wo = contract_first(grad_attn_all, gated_out)
    _, silu_pull = jax.vjp(jax.nn.silu, gate_pre)
    grad_gate = silu_pull((grad_gated * grouped).reshape(seg_len, heads_local * DV))[0].astype(
        jnp.bfloat16
    )
    retained_gradient = norm_back(grad_gated * gate_act, grouped, inv_group).astype(jnp.bfloat16)
    grad_weights = jnp.einsum(
        "thv,nhv->htn", retained_gradient, reduced_values, preferred_element_type=jnp.float32
    )
    grad_values = jnp.einsum(
        "htn,thv->nhv", weights_low, retained_gradient, preferred_element_type=jnp.float32
    )
    grad_scores = (grad_weights * decay_mat).astype(jnp.bfloat16)
    grad_q_rot = jnp.einsum(
        "htn,nhk->thk", grad_scores, rotated_keys, preferred_element_type=jnp.float32
    )
    grad_q_rot = grad_q_rot + continuation_factor[:, :, None] * jnp.einsum(
        "mjr,jwr->mjw", retained_gradient, state_lookup, preferred_element_type=jnp.float32
    )
    grad_k_rot = jnp.einsum(
        "htn,thk->nhk", grad_scores, rotated_queries, preferred_element_type=jnp.float32
    )
    state_grad_own = jnp.einsum(
        "ybn,ybw->bnw",
        rotated_queries.astype(jnp.float32) * continuation_factor[:, :, None],
        retained_gradient.astype(jnp.float32),
        precision=lax.Precision.HIGHEST,
    )
    grad_slots = group_onehot[:, None, None, None] * state_grad_own[None]
    grad_summed = lax.psum(grad_slots, "dp")
    state_gradient = (
        prompt_flag * jnp.sum(grad_summed * group_onehot[:, None, None, None], axis=0)
    ).astype(jnp.bfloat16)
    grad_k_rot = grad_k_rot + state_weighting[:, :, None] * jnp.einsum(
        "ilm,lpm->ilp", reduced_values, state_gradient, preferred_element_type=jnp.float32
    )
    grad_values = grad_values + state_weighting[:, :, None] * jnp.einsum(
        "zdo,doi->zdi", rotated_keys, state_gradient, preferred_element_type=jnp.float32
    )
    grad_queries = (
        rotate_back(grad_q_rot * q_scale, cosine, sine_tab, grow_fac)
        .reshape(seg_len, heads_local * DK)
        .astype(jnp.bfloat16)
    )
    grad_keys = (
        rotate_back(grad_k_rot, cosine, sine_tab, shrink)
        .reshape(seg_len, heads_local * DK)
        .astype(jnp.bfloat16)
    )
    grad_vlow = grad_values.reshape(seg_len, heads_local * DV).astype(jnp.bfloat16)
    grad_wq = contract_first(a_all, grad_queries)
    grad_wk = contract_first(a_all, grad_keys)
    grad_wv = contract_first(a_all, grad_vlow)
    grad_wg = contract_first(a_all, grad_gate)
    grad_a_terms = (
        contract_last(grad_queries, wq_full)
        + contract_last(grad_keys, wk_full)
        + contract_last(grad_vlow, wv_full)
        + contract_last(grad_gate, wg_full)
    )
    grad_a = scatter_rows(grad_a_terms)
    grad_gain1_part = jnp.sum(grad_a * normed_one, axis=0)
    grad_bias1_part = jnp.sum(grad_a, axis=0)
    grad_tokens = grad_hidden + norm_back(grad_a * gain_one, normed_one, inv_one)
    attn_reduced = (
        lax.psum_scatter(grad_gain1_part, "dp", scatter_dimension=0, tiled=True),
        lax.psum_scatter(grad_bias1_part, "dp", scatter_dimension=0, tiled=True),
        lax.psum_scatter(grad_wq, "dp", scatter_dimension=0, tiled=True),
        lax.psum_scatter(grad_wk, "dp", scatter_dimension=0, tiled=True),
        lax.psum_scatter(grad_wv, "dp", scatter_dimension=0, tiled=True),
        lax.psum_scatter(grad_wg, "dp", scatter_dimension=0, tiled=True),
        lax.psum_scatter(grad_wo, "dp", scatter_dimension=0, tiled=True),
    )
    norm_sums = lax.psum((attn_reduced[0], attn_reduced[1], ffn_reduced[0], ffn_reduced[1]), "mp")
    return (
        block_out,
        grad_tokens,
        loss_value,
        norm_sums[0],
        norm_sums[1],
        attn_reduced[2],
        attn_reduced[3],
        attn_reduced[4],
        attn_reduced[5],
        attn_reduced[6],
        norm_sums[2],
        norm_sums[3],
        ffn_reduced[2],
        ffn_reduced[3],
    )


def solution(mesh):
    return jax.shard_map(
        on_device,
        mesh=mesh,
        in_specs=(
            P(("dp", "mp"), None),
            P(("dp", "mp"), None),
            P("dp", "mp"),
            P(),
            P(),
            P("dp"),
            P("dp"),
            P("dp", "mp"),
            P("dp", "mp"),
            P("dp", "mp"),
            P("dp", "mp"),
            P("dp", "mp"),
            P("dp"),
            P("dp"),
            P("dp", "mp"),
            P("dp", "mp"),
        ),
        out_specs=(
            P(("dp", "mp"), None),
            P(("dp", "mp"), None),
            P(),
            P("dp"),
            P("dp"),
            P("dp", "mp"),
            P("dp", "mp"),
            P("dp", "mp"),
            P("dp", "mp"),
            P("dp", "mp"),
            P("dp"),
            P("dp"),
            P("dp", "mp"),
            P("dp", "mp"),
        ),
        check_vma=False,
    )
```

profile of v0, /device:TPU:0, one launch (start us, length us, event | category | flops | bytes accessed | tf_op | source)
XLA Modules:
  0.0 2218.7 jit_solution(17705684298100000474)
XLA Ops:
  9.8 23.3 %all-gather = bf16[16,1,128]{2,1,0:T(2,128)(2,1)S(1)} all-gather(bf16[1,1,128]{2,1,0:T(2,128)(2,1)} %bitcast.140), channel_id=1, replica_groups=mesh['dp'=16,'mp'=2] {'dp'}, dimensions={0}, use_global_device_ids=true | all-gather | bytes 4352 | tf_op jit(solution)/shard_map/all_gather | solution.py:120
  72.8 52.6 %all-gather.24.cloned.1.call-done = bf16[2048,1024]{1,0:T(8,128)(2,1)} async-done(((bf16[128,1024]{1,0:T(8,128)(2,1)}), bf16[2048,1024]{1,0:T(8,128)(2,1)}) %all-gather.24.cloned.1.call-update) | async-done | bytes 4194320 | tf_op jit(solution)/shard_map/all_gather | solution.py:123
  129.7 46.8 %all-gather.22.cloned.1.call-done = bf16[2048,1024]{1,0:T(8,128)(2,1)} async-done(((bf16[128,1024]{1,0:T(8,128)(2,1)}), bf16[2048,1024]{1,0:T(8,128)(2,1)}) %all-gather.22.cloned.1.call-update) | async-done | bytes 4194320 | tf_op jit(solution)/shard_map/all_gather | solution.py:122
  185.0 66.4 %all-gather.20.cloned.1.call-done = bf16[2048,2048]{1,0:T(8,128)(2,1)} async-done(((bf16[128,2048]{1,0:T(8,128)(2,1)}), bf16[2048,2048]{1,0:T(8,128)(2,1)}) %all-gather.20.cloned.1.call-update) | async-done | bytes 8388624 | tf_op jit(solution)/shard_map/all_gather | solution.py:124
  265.3 61.1 %all-gather.18.cloned.1.call-done = bf16[2048,2048]{1,0:T(8,128)(2,1)} async-done(((bf16[128,2048]{1,0:T(8,128)(2,1)}), bf16[2048,2048]{1,0:T(8,128)(2,1)}) %all-gather.18.cloned.1.call-update) | async-done | bytes 8388624 | tf_op jit(solution)/shard_map/all_gather | solution.py:125
  339.0 100.7 %all-reduce.10.cloned.1.call-done = f32[2,4,256,512]{3,2,1,0:T(8,128)} async-done(((f32[2,4,256,512]{3,2,1,0:T(8,128)}), f32[2,4,256,512]{3,2,1,0:T(8,128)}) %all-reduce.10.cloned.1.call-update) | async-done | bytes 4194320 | tf_op jit(solution)/shard_map/psum | solution.py:204
  445.8 69.5 %all-gather.26.cloned.1.call-done = bf16[2048,2048]{1,0:T(8,128)(2,1)} async-done(((bf16[128,2048]{1,0:T(8,128)(2,1)}), bf16[2048,2048]{1,0:T(8,128)(2,1)}) %all-gather.26.cloned.1.call-update) | async-done | bytes 8388624 | tf_op jit(solution)/shard_map/all_gather | solution.py:126
  523.2 19.0 all-gather.2
  564.7 64.9 %all-gather.30.cloned.1.call-done = bf16[2048,2048]{1,0:T(8,128)(2,1)} async-done(((bf16[128,2048]{1,0:T(8,128)(2,1)}), bf16[2048,2048]{1,0:T(8,128)(2,1)}) %all-gather.30.cloned.1.call-update) | async-done | bytes 8388624 | tf_op jit(solution)/shard_map/all_gather | solution.py:131
  629.6 21.9 all-gather.28.cloned.1.call-done
  662.1 65.9 %all-gather.32.cloned.1.call-done = bf16[2048,2048]{1,0:T(8,128)(2,1)} async-done(((bf16[128,2048]{1,0:T(8,128)(2,1)}), bf16[2048,2048]{1,0:T(8,128)(2,1)}) %all-gather.32.cloned.1.call-update) | async-done | bytes 8388624 | tf_op jit(solution)/shard_map/all_gather | solution.py:132
  737.8 28.2 %reduce-scatter.14.cloned.1.call-done = f32[128,2048]{1,0:T(8,128)} async-done(((f32[256,2048]{1,0:T(8,128)}), f32[128,2048]{1,0:T(8,128)}) %reduce-scatter.14.cloned.1.call-update) | async-done | bytes 1048592 | tf_op jit(solution)/shard_map/reduce_scatter | solution.py:89
  769.2 39.5 %all-reduce.4 = (f32[]{:T(128)}, f32[]{:T(128)}) all-reduce(f32[]{:T(128)} %get-tuple-element.39, f32[]{:T(128)} %get-tuple-element.37), channel_id=1, replica_groups=mesh['dp'=16,'mp'=2] {'dp','mp'}, use_global_device_ids=true, to_apply=%region_14.15 | all-reduce | flops 2 | bytes 16 | tf_op jit(solution)/shard_map/psum | solution.py:230
  811.9 22.3 %all-gather.34.cloned.1.call-done = bf16[256,2048]{1,0:T(8,128)(2,1)} async-done(((bf16[128,2048]{1,0:T(8,128)(2,1)}), bf16[256,2048]{1,0:T(8,128)(2,1)}) %all-gather.34.cloned.1.call-update) | async-done | bytes 1048592 | tf_op jit(solution)/shard_map/all_gather | solution.py:85
  850.2 31.8 %reduce-scatter.16.cloned.1.call-done = f32[128,2048]{1,0:T(8,128)} async-done(((f32[256,2048]{1,0:T(8,128)}), f32[128,2048]{1,0:T(8,128)}) %reduce-scatter.16.cloned.1.call-update) | async-done | bytes 1048592 | tf_op jit(solution)/shard_map/reduce_scatter | solution.py:89
  887.6 21.4 all-gather.36.cloned.1.call-done
  936.8 98.4 %all-reduce.12.cloned.1.call-done = f32[2,4,256,512]{3,2,1,0:T(8,128)} async-done(((f32[2,4,256,512]{3,2,1,0:T(8,128)}), f32[2,4,256,512]{3,2,1,0:T(8,128)}) %all-reduce.12.cloned.1.call-update) | async-done | bytes 4194320 | tf_op jit(solution)/shard_map/psum | solution.py:282
  1124.5 62.8 %all-reduce.5 = (f32[2048]{0:T(1024)S(1)}, f32[2048]{0:T(1024)S(1)}, f32[2048]{0:T(1024)S(1)}, f32[2048]{0:T(1024)S(1)}) all-reduce(f32[2048]{0:T(1024)S(1)} %get-tuple-element.18, f32[2048]{0:T(1024)S(1)} %get-tuple-element.23, f32[2048]{0:T(1024)S(1)} %copy-done.51, ...), channel_id=6, replica_groups=mesh['dp'=16,'mp'=2] {'dp'}, use_global_device_ids=true, to_apply=%region_28.29.clone | all-reduce | flops 8192 | bytes 65536
  1196.8 107.8 %reduce-scatter.20.cloned.1.call-done = f32[128,1024]{1,0:T(8,128)} async-done(((f32[2048,1024]{1,0:T(8,128)}), f32[128,1024]{1,0:T(8,128)}) %reduce-scatter.20.cloned.1.call-update) | async-done | bytes 524304 | tf_op jit(solution)/shard_map/reduce_scatter | solution.py:320
  1304.6 181.5 %reduce-scatter.30.cloned.1.call-done = f32[128,2048]{1,0:T(8,128)} async-done(((f32[2048,2048]{1,0:T(8,128)}), f32[128,2048]{1,0:T(8,128)}) %reduce-scatter.30.cloned.1.call-update) | async-done | bytes 1048592 | tf_op jit(solution)/shard_map/reduce_scatter | solution.py:248
  1486.1 181.1 %reduce-scatter.32.cloned.1.call-done = f32[128,2048]{1,0:T(8,128)} async-done(((f32[2048,2048]{1,0:T(8,128)}), f32[128,2048]{1,0:T(8,128)}) %reduce-scatter.32.cloned.1.call-update) | async-done | bytes 1048592 | tf_op jit(solution)/shard_map/reduce_scatter | solution.py:249
  1667.3 181.1 %reduce-scatter.28.cloned.1.call-done = f32[128,2048]{1,0:T(8,128)} async-done(((f32[2048,2048]{1,0:T(8,128)}), f32[128,2048]{1,0:T(8,128)}) %reduce-scatter.28.cloned.1.call-update) | async-done | bytes 1048592 | tf_op jit(solution)/shard_map/reduce_scatter | solution.py:324
  1848.4 181.1 %reduce-scatter.26.cloned.1.call-done = f32[128,2048]{1,0:T(8,128)} async-done(((f32[2048,2048]{1,0:T(8,128)}), f32[128,2048]{1,0:T(8,128)}) %reduce-scatter.26.cloned.1.call-update) | async-done | bytes 1048592 | tf_op jit(solution)/shard_map/reduce_scatter | solution.py:323
  2029.5 181.0 %reduce-scatter.24.cloned.1.call-done = f32[128,2048]{1,0:T(8,128)} async-done(((f32[2048,2048]{1,0:T(8,128)}), f32[128,2048]{1,0:T(8,128)}) %reduce-scatter.24.cloned.1.call-update) | async-done | bytes 1048592 | tf_op jit(solution)/shard_map/reduce_scatter | solution.py:322
  (307 shorter events, 287.3 us)
Async XLA Ops:
  7.2 65.6 %all-gather.16.cloned.1.call-start = ((), (), s32[]{:S(2)}) async-start(), calls=%async_computation.11 | async-start | bytes 1572864 | tf_op jit(solution)/shard_map/all_gather | solution.py:85
  53.1 72.4 %all-gather.24.cloned.1.call-start = ((), (), s32[]{:S(2)}) async-start(), calls=%async_computation.15 | async-start | bytes 4456448 | tf_op jit(solution)/shard_map/all_gather | solution.py:123
  53.8 122.7 %all-gather.22.cloned.1.call-start = ((), (), s32[]{:S(2)}) async-start(), calls=%async_computation.14 | async-start | bytes 4456448 | tf_op jit(solution)/shard_map/all_gather | solution.py:122
  54.5 196.9 %all-gather.20.cloned.1.call-start = ((), (), s32[]{:S(2)}) async-start(), calls=%async_computation.13 | async-start | bytes 8912896 | tf_op jit(solution)/shard_map/all_gather | solution.py:124
  55.1 271.2 %all-gather.18.cloned.1.call-start = ((), (), s32[]{:S(2)}) async-start(), calls=%async_computation.12 | async-start | bytes 8912896 | tf_op jit(solution)/shard_map/all_gather | solution.py:125
  55.7 384.0 %all-reduce.10.cloned.1.call-start = ((), (), s32[]{:S(2)}) async-start(), calls=%async_computation.16 | async-start | bytes 8388608 | tf_op jit(solution)/shard_map/psum | solution.py:204
  261.1 254.1 %all-gather.26.cloned.1.call-start = ((), (), s32[]{:S(2)}) async-start(), calls=%async_computation.17 | async-start | bytes 8912896 | tf_op jit(solution)/shard_map/all_gather | solution.py:126
  261.9 298.4 %reduce-scatter.12.cloned.1.call-start = ((), (), s32[]{:S(2)}) async-start(), calls=%async_computation.18 | async-start | bytes 3145728 | tf_op jit(solution)/shard_map/reduce_scatter | solution.py:89
  522.4 107.2 %all-gather.30.cloned.1.call-start = ((), (), s32[]{:S(2)}) async-start(), calls=%async_computation.20 | async-start | bytes 8912896 | tf_op jit(solution)/shard_map/all_gather | solution.py:131
  523.2 128.3 %all-gather.28.cloned.1.call-start = ((), (), s32[]{:S(2)}) async-start(), calls=%async_computation.19 | async-start | bytes 1572864 | tf_op jit(solution)/shard_map/all_gather | solution.py:85
  563.7 164.2 %all-gather.32.cloned.1.call-start = ((), (), s32[]{:S(2)}) async-start(), calls=%async_computation.21 | async-start | bytes 8912896 | tf_op jit(solution)/shard_map/all_gather | solution.py:132
  564.5 201.6 %reduce-scatter.14.cloned.1.call-start = ((), (), s32[]{:S(2)}) async-start(), calls=%async_computation.22 | async-start | bytes 3145728 | tf_op jit(solution)/shard_map/reduce_scatter | solution.py:89
  735.4 98.8 %all-gather.34.cloned.1.call-start = ((), (), s32[]{:S(2)}) async-start(), calls=%async_computation.23 | async-start | bytes 1572864 | tf_op jit(solution)/shard_map/all_gather | solution.py:85
  811.8 70.2 %reduce-scatter.16.cloned.1.call-start = ((), (), s32[]{:S(2)}) async-start(), calls=%async_computation.24 | async-start | bytes 3145728 | tf_op jit(solution)/shard_map/reduce_scatter | solution.py:89
  850.0 59.0 %all-gather.36.cloned.1.call-start = ((), (), s32[]{:S(2)}) async-start(), calls=%async_computation.25 | async-start | bytes 1572864 | tf_op jit(solution)/shard_map/all_gather | solution.py:85
  887.6 147.5 %all-reduce.12.cloned.1.call-start = ((), (), s32[]{:S(2)}) async-start(), calls=%async_computation.26 | async-start | bytes 8388608 | tf_op jit(solution)/shard_map/psum | solution.py:282
  923.8 198.8 %reduce-scatter.18.cloned.1.call-start = ((), (), s32[]{:S(2)}) async-start(), calls=%async_computation.27 | async-start | bytes 3145728 | tf_op jit(solution)/shard_map/reduce_scatter | solution.py:89
  1056.9 139.8 %reduce-scatter.22.cloned.1.call-start = ((), (), s32[]{:S(2)}) async-start(), calls=%async_computation.29 | async-start | bytes 8912896 | tf_op jit(solution)/shard_map/reduce_scatter | solution.py:321
  1063.0 241.6 %reduce-scatter.20.cloned.1.call-start = ((), (), s32[]{:S(2)}) async-start(), calls=%async_computation.28 | async-start | bytes 8912896 | tf_op jit(solution)/shard_map/reduce_scatter | solution.py:320
  1067.7 418.4 %reduce-scatter.30.cloned.1.call-start = ((), (), s32[]{:S(2)}) async-start(), calls=%async_computation.33 | async-start | bytes 17825792 | tf_op jit(solution)/shard_map/reduce_scatter | solution.py:248
  1078.3 589.0 %reduce-scatter.32.cloned.1.call-start = ((), (), s32[]{:S(2)}) async-start(), calls=%async_computation.34 | async-start | bytes 17825792 | tf_op jit(solution)/shard_map/reduce_scatter | solution.py:249
  1088.9 759.5 %reduce-scatter.28.cloned.1.call-start = ((), (), s32[]{:S(2)}) async-start(), calls=%async_computation.32 | async-start | bytes 17825792 | tf_op jit(solution)/shard_map/reduce_scatter | solution.py:324
  1099.9 929.6 %reduce-scatter.26.cloned.1.call-start = ((), (), s32[]{:S(2)}) async-start(), calls=%async_computation.31 | async-start | bytes 17825792 | tf_op jit(solution)/shard_map/reduce_scatter | solution.py:323
  1110.0 1100.5 %reduce-scatter.24.cloned.1.call-start = ((), (), s32[]{:S(2)}) async-start(), calls=%async_computation.30 | async-start | bytes 17825792 | tf_op jit(solution)/shard_map/reduce_scatter | solution.py:322
  (73 other events, 2311.2 us)
Sparse Core Ops, SparseCore 0:
  53.2 19.6 all-gather.15
  75.0 50.3 all-gather.23
  127.6 48.8 all-gather.21
  178.5 72.8 all-gather.19
  253.4 72.8 all-gather.17
  329.9 109.7 all-reduce.9
  441.8 73.4 all-gather.25
  522.5 30.4 reduce-scatter.11
  555.2 74.3 all-gather.29
  631.5 19.8 all-gather.27
  653.6 74.2 all-gather.31
  735.5 30.4 reduce-scatter.13
  812.0 22.1 all-gather.33
  850.1 31.8 reduce-scatter.15
  887.7 21.2 all-gather.35
  924.0 111.1 all-reduce.11
  1057.1 31.0 reduce-scatter.17
  1092.6 104.1 reduce-scatter.21
  1201.4 103.1 reduce-scatter.19
  1309.1 176.9 reduce-scatter.29
  1490.8 176.4 reduce-scatter.31
  1671.9 176.3 reduce-scatter.27
  1853.1 176.3 reduce-scatter.25
  2034.0 176.3 reduce-scatter.23
where the time goes:
time: 2230 us; the launch traced here: 2220 us
  waiting for transfers between devices  1780 us (80%)
  blocking collectives  185 us (8%)
  matrix products  155 us (7%)
  other arithmetic  51.2 us (2%)
  local copies, waits for them, and re-layouts  23 us (1%)
    reduce_scatter x1, waiting for transfers between devices, on_device(): lax.psum_scatter(grad_wu, 'dp', scatter_dimension=0, tiled=True)  182 us
    reduce_scatter x1, waiting for transfers between devices, on_device(): lax.psum_scatter(grad_wd, 'dp', scatter_dimension=0, tiled=True)  181 us
    reduce_scatter x1, waiting for transfers between devices, on_device(): lax.psum_scatter(grad_wg, 'dp', scatter_dimension=0, tiled=True)  181 us
    reduce_scatter x1, waiting for transfers between devices, on_device(): lax.psum_scatter(grad_wo, 'dp', scatter_dimension=0, tiled=True)  181 us
    reduce_scatter x1, waiting for transfers between devices, on_device(): lax.psum_scatter(grad_wv, 'dp', scatter_dimension=0, tiled=True)  181 us
    reduce_scatter x1, waiting for transfers between devices, on_device(): lax.psum_scatter(grad_wq, 'dp', scatter_dimension=0, tiled=True)  108 us
    psum x1, waiting for transfers between devices, on_device(): summed = lax.psum(slots, 'dp')  101 us
    psum x1, waiting for transfers between devices, on_device(): grad_summed = lax.psum(grad_slots, 'dp')  98.4 us
  transfers between devices with their start and end apart: 24, of which 22 were waited for; matrix products, arithmetic and copies ran while one was open for 6% of the time, Pallas kernels for 0%

commit v1 on v0

--- a/solution.py
+++ b/solution.py
@@ -8,6 +8,21 @@
 DV = 512
 EPSILON = 1e-05
 GROUP_EPSILON = 0.05
+
+
+def answer_bench(t0):
+    devs = lax.axis_size("dp")
+    step_out, val = (t0, 0)
+    while 1 << val < devs:
+        line_up = []
+        it = 0
+        while it < devs:
+            line_up.append((it, it ^ 1 << val))
+            it += 1
+        p_next = lax.ppermute(step_out, "dp", line_up)
+        step_out = step_out + p_next
+        val = val + 1
+    return step_out
 
 
 def norm_stats(values, floor_eps):
@@ -279,7 +294,7 @@
         precision=lax.Precision.HIGHEST,
     )
     grad_slots = group_onehot[:, None, None, None] * state_grad_own[None]
-    grad_summed = lax.psum(grad_slots, "dp")
+    grad_summed = answer_bench(grad_slots)
     state_gradient = (
         prompt_flag * jnp.sum(grad_summed * group_onehot[:, None, None, None], axis=0)
     ).astype(jnp.bfloat16)

time: 2230 us -> 2490 us (1.12)
  waiting for transfers between devices: 1780 us -> 2040 us
    ppermute x0 -> x4, waiting for transfers between devices: none -> 358 us  [answer_bench(): p_next = lax.ppermute(step_out, 'dp', line_up)]
    reduce_scatter x1, waiting for transfers between devices: 182 us -> 71 us  [on_device(): lax.psum_scatter(grad_wu, 'dp', scatter_dimension=0, tiled=True)]
    reduce_scatter x1, waiting for transfers between devices: 2.26 us -> 107 us  [on_device(): lax.psum_scatter(grad_wk, 'dp', scatter_dimension=0, tiled=True)]
    psum x1 -> x0, waiting for transfers between devices: 98.4 us -> none  [on_device(): grad_summed = lax.psum(grad_slots, 'dp')]
  transfers between devices with their start and end apart: 24 -> 27, of which waited for: 22 -> 25; matrix products, arithmetic and copies ran while one was open for 6% -> 5% of each run, Pallas kernels for 0% -> 0%
where the time goes in v1:
time: 2490 us
  waiting for transfers between devices  2040 us (82%)
  blocking collectives  188 us (8%)
  matrix products  155 us (6%)
  other arithmetic  55.6 us (2%)
    ppermute x4, waiting for transfers between devices, answer_bench(): p_next = lax.ppermute(step_out, 'dp', line_up)  358 us
    reduce_scatter x1, waiting for transfers between devices, on_device(): lax.psum_scatter(grad_wv, 'dp', scatter_dimension=0, tiled=True)  182 us
    reduce_scatter x1, waiting for transfers between devices, on_device(): lax.psum_scatter(grad_wo, 'dp', scatter_dimension=0, tiled=True)  181 us
    reduce_scatter x1, waiting for transfers between devices, on_device(): lax.psum_scatter(grad_wd, 'dp', scatter_dimension=0, tiled=True)  181 us
    reduce_scatter x1, waiting for transfers between devices, on_device(): lax.psum_scatter(grad_wg, 'dp', scatter_dimension=0, tiled=True)  181 us
    reduce_scatter x1, waiting for transfers between devices, on_device(): lax.psum_scatter(grad_wq, 'dp', scatter_dimension=0, tiled=True)  108 us
    reduce_scatter x1, waiting for transfers between devices, on_device(): lax.psum_scatter(grad_wk, 'dp', scatter_dimension=0, tiled=True)  107 us
    psum x1, waiting for transfers between devices, on_device(): summed = lax.psum(slots, 'dp')  101 us
  transfers between devices with their start and end apart: 27, of which 25 were waited for; matrix products, arithmetic and copies ran while one was open for 5% of the time, Pallas kernels for 0%

profile of v1, /device:TPU:0, one launch (start us, length us, event | category | flops | bytes accessed | tf_op | source)
XLA Modules:
  0.0 2486.5 jit_solution(8708698166696597339)
XLA Ops:
  9.8 23.3 all-gather
  72.8 52.6 %all-gather.24.cloned.1.call-done = bf16[2048,1024]{1,0:T(8,128)(2,1)} async-done(((bf16[128,1024]{1,0:T(8,128)(2,1)}), bf16[2048,1024]{1,0:T(8,128)(2,1)}) %all-gather.24.cloned.1.call-update) | async-done | bytes 4194320 | tf_op jit(solution)/shard_map/all_gather | solution.py:138
  129.7 46.8 %all-gather.22.cloned.1.call-done = bf16[2048,1024]{1,0:T(8,128)(2,1)} async-done(((bf16[128,1024]{1,0:T(8,128)(2,1)}), bf16[2048,1024]{1,0:T(8,128)(2,1)}) %all-gather.22.cloned.1.call-update) | async-done | bytes 4194320 | tf_op jit(solution)/shard_map/all_gather | solution.py:137
  185.0 66.4 %all-gather.20.cloned.1.call-done = bf16[2048,2048]{1,0:T(8,128)(2,1)} async-done(((bf16[128,2048]{1,0:T(8,128)(2,1)}), bf16[2048,2048]{1,0:T(8,128)(2,1)}) %all-gather.20.cloned.1.call-update) | async-done | bytes 8388624 | tf_op jit(solution)/shard_map/all_gather | solution.py:139
  265.3 61.1 %all-gather.18.cloned.1.call-done = bf16[2048,2048]{1,0:T(8,128)(2,1)} async-done(((bf16[128,2048]{1,0:T(8,128)(2,1)}), bf16[2048,2048]{1,0:T(8,128)(2,1)}) %all-gather.18.cloned.1.call-update) | async-done | bytes 8388624 | tf_op jit(solution)/shard_map/all_gather | solution.py:140
  339.0 100.7 %all-reduce.9.cloned.1.call-done = f32[2,4,256,512]{3,2,1,0:T(8,128)} async-done(((f32[2,4,256,512]{3,2,1,0:T(8,128)}), f32[2,4,256,512]{3,2,1,0:T(8,128)}) %all-reduce.9.cloned.1.call-update) | async-done | bytes 4194320 | tf_op jit(solution)/shard_map/psum | solution.py:219
  445.8 69.5 %all-gather.26.cloned.1.call-done = bf16[2048,2048]{1,0:T(8,128)(2,1)} async-done(((bf16[128,2048]{1,0:T(8,128)(2,1)}), bf16[2048,2048]{1,0:T(8,128)(2,1)}) %all-gather.26.cloned.1.call-update) | async-done | bytes 8388624 | tf_op jit(solution)/shard_map/all_gather | solution.py:141
  564.7 64.9 %all-gather.30.cloned.1.call-done = bf16[2048,2048]{1,0:T(8,128)(2,1)} async-done(((bf16[128,2048]{1,0:T(8,128)(2,1)}), bf16[2048,2048]{1,0:T(8,128)(2,1)}) %all-gather.30.cloned.1.call-update) | async-done | bytes 8388624 | tf_op jit(solution)/shard_map/all_gather | solution.py:146
  662.0 65.9 %all-gather.32.cloned.1.call-done = bf16[2048,2048]{1,0:T(8,128)(2,1)} async-done(((bf16[128,2048]{1,0:T(8,128)(2,1)}), bf16[2048,2048]{1,0:T(8,128)(2,1)}) %all-gather.32.cloned.1.call-update) | async-done | bytes 8388624 | tf_op jit(solution)/shard_map/all_gather | solution.py:147
  737.8 28.2 %reduce-scatter.14.cloned.1.call-done = f32[128,2048]{1,0:T(8,128)} async-done(((f32[256,2048]{1,0:T(8,128)}), f32[128,2048]{1,0:T(8,128)}) %reduce-scatter.14.cloned.1.call-update) | async-done | bytes 1048592 | tf_op jit(solution)/shard_map/reduce_scatter | solution.py:104
  769.2 39.5 %all-reduce.4 = (f32[]{:T(128)}, f32[]{:T(128)}) all-reduce(f32[]{:T(128)} %get-tuple-element.39, f32[]{:T(128)} %get-tuple-element.37), channel_id=1, replica_groups=mesh['dp'=16,'mp'=2] {'dp','mp'}, use_global_device_ids=true, to_apply=%region_14.15 | all-reduce | flops 2 | bytes 16 | tf_op jit(solution)/shard_map/psum | solution.py:245
  811.9 22.3 all-gather.34.cloned.1.call-done
  850.2 31.8 %reduce-scatter.16.cloned.1.call-done = f32[128,2048]{1,0:T(8,128)} async-done(((f32[256,2048]{1,0:T(8,128)}), f32[128,2048]{1,0:T(8,128)}) %reduce-scatter.16.cloned.1.call-update) | async-done | bytes 1048592 | tf_op jit(solution)/shard_map/reduce_scatter | solution.py:104
  931.5 91.1 %collective-permute-done.1 = f32[2,4,256,512]{3,2,1,0:T(8,128)S(1)} collective-permute-done((f32[2,4,256,512]{3,2,1,0:T(8,128)S(1)}, f32[2,4,256,512]{3,2,1,0:T(8,128)S(1)}, u32[]{:S(2)}, u32[]{:S(2)}) %collective-permute-start.1) | collective-permute-done | bytes 4194336 | tf_op jit(solution)/shard_map/ppermute | solution.py:22
  1025.6 90.3 %collective-permute-done.2 = f32[2,4,256,512]{3,2,1,0:T(8,128)S(1)} collective-permute-done((f32[2,4,256,512]{3,2,1,0:T(8,128)S(1)}, f32[2,4,256,512]{3,2,1,0:T(8,128)S(1)}, u32[]{:S(2)}, u32[]{:S(2)}) %collective-permute-start.2) | collective-permute-done | bytes 4194336 | tf_op jit(solution)/shard_map/ppermute | solution.py:22
  1131.5 169.3 %collective-permute-done.3 = f32[2,4,256,512]{3,2,1,0:T(8,128)} collective-permute-done((f32[2,4,256,512]{3,2,1,0:T(8,128)}, f32[2,4,256,512]{3,2,1,0:T(8,128)}, u32[]{:S(2)}, u32[]{:S(2)}) %collective-permute-start.3) | collective-permute-done | bytes 4194336 | tf_op jit(solution)/shard_map/ppermute | solution.py:22
  1394.8 65.9 %all-reduce.5 = (f32[2048]{0:T(1024)S(1)}, f32[2048]{0:T(1024)S(1)}, f32[2048]{0:T(1024)S(1)}, f32[2048]{0:T(1024)S(1)}) all-reduce(f32[2048]{0:T(1024)S(1)} %get-tuple-element.18, f32[2048]{0:T(1024)S(1)} %get-tuple-element.23, f32[2048]{0:T(1024)S(1)} %copy-done.46, ...), channel_id=6, replica_groups=mesh['dp'=16,'mp'=2] {'dp'}, use_global_device_ids=true, to_apply=%region_27.28.clone | all-reduce | flops 8192 | bytes 65536
  1467.9 71.0 %reduce-scatter.30.cloned.1.call-done = f32[128,2048]{1,0:T(8,128)} async-done(((f32[2048,2048]{1,0:T(8,128)}), f32[128,2048]{1,0:T(8,128)}) %reduce-scatter.30.cloned.1.call-update) | async-done | bytes 1048592 | tf_op jit(solution)/shard_map/reduce_scatter | solution.py:263
  1538.8 181.0 %reduce-scatter.32.cloned.1.call-done = f32[128,2048]{1,0:T(8,128)} async-done(((f32[2048,2048]{1,0:T(8,128)}), f32[128,2048]{1,0:T(8,128)}) %reduce-scatter.32.cloned.1.call-update) | async-done | bytes 1048592 | tf_op jit(solution)/shard_map/reduce_scatter | solution.py:264
  1719.8 181.1 %reduce-scatter.28.cloned.1.call-done = f32[128,2048]{1,0:T(8,128)} async-done(((f32[2048,2048]{1,0:T(8,128)}), f32[128,2048]{1,0:T(8,128)}) %reduce-scatter.28.cloned.1.call-update) | async-done | bytes 1048592 | tf_op jit(solution)/shard_map/reduce_scatter | solution.py:339
  1901.0 181.0 %reduce-scatter.26.cloned.1.call-done = f32[128,2048]{1,0:T(8,128)} async-done(((f32[2048,2048]{1,0:T(8,128)}), f32[128,2048]{1,0:T(8,128)}) %reduce-scatter.26.cloned.1.call-update) | async-done | bytes 1048592 | tf_op jit(solution)/shard_map/reduce_scatter | solution.py:338
  2081.9 107.2 %reduce-scatter.22.cloned.1.call-done = f32[128,1024]{1,0:T(8,128)} async-done(((f32[2048,1024]{1,0:T(8,128)}), f32[128,1024]{1,0:T(8,128)}) %reduce-scatter.22.cloned.1.call-update) | async-done | bytes 524304 | tf_op jit(solution)/shard_map/reduce_scatter | solution.py:336
  2189.2 107.8 %reduce-scatter.20.cloned.1.call-done = f32[128,1024]{1,0:T(8,128)} async-done(((f32[2048,1024]{1,0:T(8,128)}), f32[128,1024]{1,0:T(8,128)}) %reduce-scatter.20.cloned.1.call-update) | async-done | bytes 524304 | tf_op jit(solution)/shard_map/reduce_scatter | solution.py:335
  2296.9 181.7 %reduce-scatter.24.cloned.1.call-done = f32[128,2048]{1,0:T(8,128)} async-done(((f32[2048,2048]{1,0:T(8,128)}), f32[128,2048]{1,0:T(8,128)}) %reduce-scatter.24.cloned.1.call-update) | async-done | bytes 1048592 | tf_op jit(solution)/shard_map/reduce_scatter | solution.py:337
  (305 shorter events, 365.2 us)
Async XLA Ops:
  53.1 72.4 %all-gather.24.cloned.1.call-start = ((), (), s32[]{:S(2)}) async-start(), calls=%async_computation.15 | async-start | bytes 4456448 | tf_op jit(solution)/shard_map/all_gather | solution.py:138
  53.8 122.7 %all-gather.22.cloned.1.call-start = ((), (), s32[]{:S(2)}) async-start(), calls=%async_computation.14 | async-start | bytes 4456448 | tf_op jit(solution)/shard_map/all_gather | solution.py:137
  54.5 196.9 %all-gather.20.cloned.1.call-start = ((), (), s32[]{:S(2)}) async-start(), calls=%async_computation.13 | async-start | bytes 8912896 | tf_op jit(solution)/shard_map/all_gather | solution.py:139
  55.1 271.2 %all-gather.18.cloned.1.call-start = ((), (), s32[]{:S(2)}) async-start(), calls=%async_computation.12 | async-start | bytes 8912896 | tf_op jit(solution)/shard_map/all_gather | solution.py:140
  55.7 384.0 %all-reduce.9.cloned.1.call-start = ((), (), s32[]{:S(2)}) async-start(), calls=%async_computation.16 | async-start | bytes 8388608 | tf_op jit(solution)/shard_map/psum | solution.py:219
  261.1 254.1 %all-gather.26.cloned.1.call-start = ((), (), s32[]{:S(2)}) async-start(), calls=%async_computation.17 | async-start | bytes 8912896 | tf_op jit(solution)/shard_map/all_gather | solution.py:141
  261.9 298.4 %reduce-scatter.12.cloned.1.call-start = ((), (), s32[]{:S(2)}) async-start(), calls=%async_computation.18 | async-start | bytes 3145728 | tf_op jit(solution)/shard_map/reduce_scatter | solution.py:104
  522.4 107.2 %all-gather.30.cloned.1.call-start = ((), (), s32[]{:S(2)}) async-start(), calls=%async_computation.20 | async-start | bytes 8912896 | tf_op jit(solution)/shard_map/all_gather | solution.py:146
  523.1 128.3 %all-gather.28.cloned.1.call-start = ((), (), s32[]{:S(2)}) async-start(), calls=%async_computation.19 | async-start | bytes 1572864 | tf_op jit(solution)/shard_map/all_gather | solution.py:100
  563.7 164.2 %all-gather.32.cloned.1.call-start = ((), (), s32[]{:S(2)}) async-start(), calls=%async_computation.21 | async-start | bytes 8912896 | tf_op jit(solution)/shard_map/all_gather | solution.py:147
  564.4 201.6 %reduce-scatter.14.cloned.1.call-start = ((), (), s32[]{:S(2)}) async-start(), calls=%async_computation.22 | async-start | bytes 3145728 | tf_op jit(solution)/shard_map/reduce_scatter | solution.py:104
  735.4 98.8 %all-gather.34.cloned.1.call-start = ((), (), s32[]{:S(2)}) async-start(), calls=%async_computation.23 | async-start | bytes 1572864 | tf_op jit(solution)/shard_map/all_gather | solution.py:100
  811.8 70.2 %reduce-scatter.16.cloned.1.call-start = ((), (), s32[]{:S(2)}) async-start(), calls=%async_computation.24 | async-start | bytes 3145728 | tf_op jit(solution)/shard_map/reduce_scatter | solution.py:104
  887.6 505.4 %reduce-scatter.18.cloned.1.call-start = ((), (), s32[]{:S(2)}) async-start(), calls=%async_computation.26 | async-start | bytes 3145728 | tf_op jit(solution)/shard_map/reduce_scatter | solution.py:104
  930.0 92.7 %collective-permute-start.1 = (f32[2,4,256,512]{3,2,1,0:T(8,128)S(1)}, f32[2,4,256,512]{3,2,1,0:T(8,128)S(1)}, u32[]{:S(2)}, u32[]{:S(2)}) collective-permute-start(f32[2,4,256,512]{3,2,1,0:T(8,128)S(1)} %fusion.56), channel_id=1, source_target_pairs={{0,4},{2,6},{4,0},{6,2},{8,12},{10,14},{12,8},{14,10},{16,20},{18,... | collective-permute-start | bytes 12582920 | tf_op jit(solution)/shard_map/ppermute | solution.py:22
  1024.0 91.8 %collective-permute-start.2 = (f32[2,4,256,512]{3,2,1,0:T(8,128)S(1)}, f32[2,4,256,512]{3,2,1,0:T(8,128)S(1)}, u32[]{:S(2)}, u32[]{:S(2)}) collective-permute-start(f32[2,4,256,512]{3,2,1,0:T(8,128)S(1)} %fusion.140), channel_id=1, source_target_pairs={{0,8},{2,10},{4,12},{6,14},{8,0},{10,2},{12,4},{14,6},{16,24},{18,... | collective-permute-start | bytes 12582920 | tf_op jit(solution)/shard_map/ppermute | solution.py:22
  1118.8 182.0 %collective-permute-start.3 = (f32[2,4,256,512]{3,2,1,0:T(8,128)}, f32[2,4,256,512]{3,2,1,0:T(8,128)}, u32[]{:S(2)}, u32[]{:S(2)}) collective-permute-start(f32[2,4,256,512]{3,2,1,0:T(8,128)} %add.239), channel_id=1, source_target_pairs={{0,16},{2,18},{4,20},{6,22},{8,24},{10,26},{12,28},{14,30},{16,0},... | collective-permute-start | bytes 12582920 | tf_op jit(solution)/shard_map/ppermute | solution.py:22
  1324.2 214.6 %reduce-scatter.30.cloned.1.call-start = ((), (), s32[]{:S(2)}) async-start(), calls=%async_computation.32 | async-start | bytes 17825792 | tf_op jit(solution)/shard_map/reduce_scatter | solution.py:263
  1335.3 384.5 %reduce-scatter.32.cloned.1.call-start = ((), (), s32[]{:S(2)}) async-start(), calls=%async_computation.33 | async-start | bytes 17825792 | tf_op jit(solution)/shard_map/reduce_scatter | solution.py:264
  1345.9 555.0 %reduce-scatter.28.cloned.1.call-start = ((), (), s32[]{:S(2)}) async-start(), calls=%async_computation.31 | async-start | bytes 17825792 | tf_op jit(solution)/shard_map/reduce_scatter | solution.py:339
  1356.5 725.4 %reduce-scatter.26.cloned.1.call-start = ((), (), s32[]{:S(2)}) async-start(), calls=%async_computation.30 | async-start | bytes 17825792 | tf_op jit(solution)/shard_map/reduce_scatter | solution.py:338
  1366.1 823.1 %reduce-scatter.22.cloned.1.call-start = ((), (), s32[]{:S(2)}) async-start(), calls=%async_computation.28 | async-start | bytes 8912896 | tf_op jit(solution)/shard_map/reduce_scatter | solution.py:336
  1372.3 924.7 %reduce-scatter.20.cloned.1.call-start = ((), (), s32[]{:S(2)}) async-start(), calls=%async_computation.27 | async-start | bytes 8912896 | tf_op jit(solution)/shard_map/reduce_scatter | solution.py:335
  1378.2 1100.5 %reduce-scatter.24.cloned.1.call-start = ((), (), s32[]{:S(2)}) async-start(), calls=%async_computation.29 | async-start | bytes 17825792 | tf_op jit(solution)/shard_map/reduce_scatter | solution.py:337
  (71 other events, 2404.6 us)
Sparse Core Ops, SparseCore 0:
  53.2 19.6 all-gather.15
  75.0 50.3 all-gather.23
  127.6 48.8 all-gather.21
  178.5 72.8 all-gather.19
  253.4 72.8 all-gather.17
  329.9 109.7 all-reduce.8
  441.8 73.4 all-gather.25
  522.5 30.4 reduce-scatter.11
  555.2 74.3 all-gather.29
  631.5 19.8 all-gather.27
  653.6 74.2 all-gather.31
  735.5 30.4 reduce-scatter.13
  811.9 22.1 all-gather.33
  850.1 31.8 reduce-scatter.15
  887.7 21.2 all-gather.35
  1324.3 31.8 reduce-scatter.17
  1360.8 177.9 reduce-scatter.29
  1543.4 176.4 reduce-scatter.31
  1724.5 176.4 reduce-scatter.27
  1905.5 176.4 reduce-scatter.25
  2086.6 102.5 reduce-scatter.21
  2193.8 103.0 reduce-scatter.19
  2301.6 176.9 reduce-scatter.23
